TPU v7x, 256 devices: a whole 4x4x8 slice. The times are simulated.
256 devices in a mesh: chain: 4 (over z_lo, core), mesh: 16 (over z_hi, y), probe: 4 (over x).
Axes of the slice: x: 4, y: 4, z: 8 (z_hi: 4, z_lo: 2; z = z_hi * 2 + z_lo), core: 2. Of those that a mesh axis runs over, the one named last changes fastest.
Arguments:
- signs: int32 [256, 8, 4096], P('probe', 'chain', 'mesh'), may hold values from 0 to 1
- border_signs: int32 [256, 512], P('probe'), may hold values from 0 to 1
- inverse_factors: bfloat16 [8, 4096, 4096], P('chain', 'mesh'), may hold values from -2 to 2, as said below
- couplings: bfloat16 [8, 32, 4, 128, 128], P('chain', 'mesh'), may hold values from -0.15625 to 0.15625
- coupling_cols: int32 [8, 32, 4], P('chain', 'mesh'), may hold values from 0 to 31, all different within a row
- border_rows: bfloat16 [8, 512, 4096], P('chain', None, 'mesh'), may hold values from -0.046875 to 0.046875
- border_inverse: bfloat16 [512, 512], replicated, may hold values from -2 to 2, as said below
Outputs:
- solved: bfloat16 [256, 8, 4096], P('probe', 'chain', 'mesh')
- border_solved: float32 [256, 512], P('probe')
- node_var: float32 [8, 4096], P('chain', 'mesh')
- border_var: float32 [512], replicated
Inputs may be any that keep to these rules, and one draw needn't show every extreme that they name: `inverse_factors`: lower triangular; diagonal entries between 0.5 and 2. `border_inverse`: lower triangular; diagonal entries between 0.5 and 2. `coupling_cols`: the 4 block columns of one block row differ.
All inputs are finite; a program needn't handle non-finite values.
Results may differ from a plain program's by a relative error of at most 0.015.
Values may be sent and summed in bfloat16 or wider, within the bound.
No kernel may reach another device: no remote copies, remote signals or barrier semaphores. Data moves between devices by JAX's collectives and lax.ppermute only.
A program may use at most 64 MiB of HBM per device.

v0:
```python
import jax
import jax.numpy as jnp
from jax import lax
from jax.sharding import PartitionSpec as P


def as_sent(shard):
    return jax.tree.map(lambda a: a.astype(jnp.bfloat16) if a.dtype == jnp.float32 else a, shard)


def shifted(value, axis, steps):
    count = lax.axis_size(axis)
    first, last = (max(0, -steps), min(count, count - steps))
    return lax.ppermute(value, axis, [(source, source + steps) for source in range(first, last)])


def apply_inverse(factor, piece):
    return lax.dot_general(
        piece, factor, (((1,), (1,)), ((), ())), preferred_element_type=jnp.float32
    )


def shards(
    signs, border_signs, inverse_factors, couplings, coupling_cols, border_rows, border_inverse
):
    probes, steps, local = signs.shape
    width = inverse_factors.shape[2]
    block = couplings.shape[3]
    source = (2 * signs - 1).astype(jnp.float32)
    border_source = (2 * border_signs - 1).astype(jnp.float32)

    def coupled_term(prev, step):
        blocks = prev.reshape(probes, width // block, block)[:, coupling_cols[step]]
        term = jnp.einsum(
            "prkc,rkdc->prd", blocks, couplings[step], preferred_element_type=jnp.float32
        )
        return term.reshape(probes, local)

    def sweep(prev):
        outputs = []
        for step in range(steps):
            resid_b = (source[:, step] - coupled_term(prev, step)).astype(jnp.bfloat16)
            solved_now = apply_inverse(
                inverse_factors[step], lax.all_gather(resid_b, "mesh", axis=1, tiled=True)
            ).astype(jnp.bfloat16)
            outputs.append(solved_now)
            if step + 1 < steps:
                prev = lax.all_gather(solved_now, "mesh", axis=1, tiled=True)
        return outputs

    def turn(index, carry):
        prev, unused = carry
        outputs = sweep(prev)
        last = outputs[-1]
        moved = jax.tree.map(
            lambda part, own: part.astype(own.dtype), shifted(as_sent(last), "chain", 1), last
        )
        incoming = jax.tree.map(
            lambda part, own: part.astype(own.dtype),
            lax.all_gather(as_sent(moved), "mesh", axis=1, tiled=True),
            moved,
        )
        return (incoming, jnp.stack(outputs, axis=1))

    start_prev = jnp.zeros((probes, width), jnp.bfloat16)
    start_out = jnp.zeros((probes, steps, local), jnp.bfloat16)
    final_prev, solved = lax.fori_loop(0, lax.axis_size("chain"), turn, (start_prev, start_out))
    partial_border = jnp.zeros((probes, border_rows.shape[1]), jnp.float32)
    for step in range(steps):
        partial_border = partial_border + lax.dot_general(
            solved[:, step],
            border_rows[step],
            (((1,), (1,)), ((), ())),
            preferred_element_type=jnp.float32,
        )
    coupled_border = lax.psum(lax.psum(partial_border, "mesh"), "chain")
    border_resid = (border_source - coupled_border).astype(jnp.bfloat16)
    border_solved = lax.dot_general(
        border_resid, border_inverse, (((1,), (1,)), ((), ())), preferred_element_type=jnp.float32
    )
    total_probes = probes * lax.axis_size("probe")
    node_sums = jnp.sum(jnp.square(solved.astype(jnp.float32)), axis=0)
    node_var = lax.psum(node_sums, "probe") / total_probes
    border_var = lax.psum(jnp.sum(jnp.square(border_solved), axis=0), "probe") / total_probes
    return (solved, border_solved, node_var, border_var)


def solution(mesh):
    return jax.shard_map(
        shards,
        mesh=mesh,
        in_specs=(
            P("probe", "chain", "mesh"),
            P("probe", None),
            P("chain", "mesh", None),
            P("chain", "mesh", None, None, None),
            P("chain", "mesh", None),
            P("chain", None, "mesh"),
            P(),
        ),
        out_specs=(P("probe", "chain", "mesh"), P("probe", None), P("chain", "mesh"), P()),
        check_vma=False,
    )
```

profile of v0, /device:TPU:1, one launch (start us, length us, event | category | flops | bytes accessed | tf_op | source)
XLA Modules:
  0.0 972.4 jit_solution(17167018165982769261)
XLA Ops:
  7.2 1.0 fusion.24
  8.3 735.5 %while.12 = (s32[]{:T(128)}, bf16[64,4096]{1,0:T(8,128)(2,1)S(1)}, bf16[64,2,256]{2,0,1:T(8,128)(2,1)}, f32[64,2,256]{2,0,1:T(8,128)S(1)}, s32[2,2,4]{2,1,0:T(2,...) while((s32[]{:T(128)}, bf16[64,4096]{1,0:T(8,128)(2,1)S(1)}, ...), condition=%wide.region_1.0_spmd, body=%wide.region_0.0_spmd.sunk | while | flops 302123072 | bytes 13771289 | solution.py:67
  8.3 0.8 compare_select_fusion.3
  10.0 1.2 convolution_bitcast_fusion.4
  11.2 43.4 %all_gather.16 = bf16[64,4096]{1,0:T(8,128)(2,1)S(1)} all-gather(bf16[64,256]{1,0:T(8,128)(2,1)S(1)} %fusion.65), channel_id=1, replica_groups=mesh['chain'=4,'mesh'=16,'probe'=4] {'mesh'}, dimensions={1}, use_global_device_ids=true | all-gather | bytes 557056 | tf_op jit(solution)/shard_map/while/body/eval_jaxpr/all_gather | solution.py:44
  54.6 2.3 fusion.66
  56.9 36.1 %all_gather.17 = bf16[64,4096]{1,0:T(8,128)(2,1)S(1)} all-gather(bf16[64,256]{1,0:T(8,128)(2,1)S(1)} %fusion.66), channel_id=1, replica_groups=mesh['chain'=4,'mesh'=16,'probe'=4] {'mesh'}, dimensions={1}, use_global_device_ids=true | all-gather | bytes 557056 | tf_op jit(solution)/shard_map/while/body/eval_jaxpr/all_gather | solution.py:48
  94.0 36.1 %all_gather.18 = bf16[64,4096]{1,0:T(8,128)(2,1)S(1)} all-gather(bf16[64,256]{1,0:T(8,128)(2,1)S(1)} %fusion.67), channel_id=1, replica_groups=mesh['chain'=4,'mesh'=16,'probe'=4] {'mesh'}, dimensions={1}, use_global_device_ids=true | all-gather | bytes 557056 | tf_op jit(solution)/shard_map/while/body/eval_jaxpr/all_gather | solution.py:44
  130.1 2.3 fusion.68
  132.4 24.8 %collective-permute-start = (bf16[64,256]{1,0:T(8,128)(2,1)S(1)}, bf16[64,256]{1,0:T(8,128)(2,1)S(1)}, u32[]{:S(2)}, u32[]{:S(2)}) collective-permute-start(bf16[64,256]{1,0:T(8,128)(2,1)S(1)} %fusion.68), channel_id=1, source_target_pairs={{0,64},{64,128},{128,192},{1,65},{65,129},{129,193},{2,66},{66,130... | collective-permute-start | bytes 98312 | tf_op jit(solution)/shard_map/while/body/eval_jaxpr/ppermute | solution.py:14
  157.2 0.6 pad_maximum_fusion.2
  158.2 36.7 %all_gather.19 = bf16[64,4096]{1,0:T(8,128)(2,1)S(1)} all-gather(bf16[64,256]{1,0:T(8,128)(2,1)S(1)} %collective-permute-done), channel_id=1, replica_groups=mesh['chain'=4,'mesh'=16,'probe'=4] {'mesh'}, dimensions={1}, use_global_device_ids=true | all-gather | bytes 557056 | tf_op jit(solution)/shard_map/while/body/eval_jaxpr/all_gather | solution.py:60
  194.9 0.8 compare_select_fusion.3
  196.6 1.2 convolution_bitcast_fusion.4
  197.8 36.6 %all_gather.16 = bf16[64,4096]{1,0:T(8,128)(2,1)S(1)} all-gather(bf16[64,256]{1,0:T(8,128)(2,1)S(1)} %fusion.65), channel_id=1, replica_groups=mesh['chain'=4,'mesh'=16,'probe'=4] {'mesh'}, dimensions={1}, use_global_device_ids=true | all-gather | bytes 557056 | tf_op jit(solution)/shard_map/while/body/eval_jaxpr/all_gather | solution.py:44
  234.4 2.3 fusion.66
  236.7 34.4 %all_gather.17 = bf16[64,4096]{1,0:T(8,128)(2,1)S(1)} all-gather(bf16[64,256]{1,0:T(8,128)(2,1)S(1)} %fusion.66), channel_id=1, replica_groups=mesh['chain'=4,'mesh'=16,'probe'=4] {'mesh'}, dimensions={1}, use_global_device_ids=true | all-gather | bytes 557056 | tf_op jit(solution)/shard_map/while/body/eval_jaxpr/all_gather | solution.py:48
  272.1 35.9 %all_gather.18 = bf16[64,4096]{1,0:T(8,128)(2,1)S(1)} all-gather(bf16[64,256]{1,0:T(8,128)(2,1)S(1)} %fusion.67), channel_id=1, replica_groups=mesh['chain'=4,'mesh'=16,'probe'=4] {'mesh'}, dimensions={1}, use_global_device_ids=true | all-gather | bytes 557056 | tf_op jit(solution)/shard_map/while/body/eval_jaxpr/all_gather | solution.py:44
  308.0 2.3 fusion.68
  310.4 30.0 %collective-permute-start = (bf16[64,256]{1,0:T(8,128)(2,1)S(1)}, bf16[64,256]{1,0:T(8,128)(2,1)S(1)}, u32[]{:S(2)}, u32[]{:S(2)}) collective-permute-start(bf16[64,256]{1,0:T(8,128)(2,1)S(1)} %fusion.68), channel_id=1, source_target_pairs={{0,64},{64,128},{128,192},{1,65},{65,129},{129,193},{2,66},{66,130... | collective-permute-start | bytes 98312 | tf_op jit(solution)/shard_map/while/body/eval_jaxpr/ppermute | solution.py:14
  340.4 0.6 pad_maximum_fusion.2
  341.4 35.2 %all_gather.19 = bf16[64,4096]{1,0:T(8,128)(2,1)S(1)} all-gather(bf16[64,256]{1,0:T(8,128)(2,1)S(1)} %collective-permute-done), channel_id=1, replica_groups=mesh['chain'=4,'mesh'=16,'probe'=4] {'mesh'}, dimensions={1}, use_global_device_ids=true | all-gather | bytes 557056 | tf_op jit(solution)/shard_map/while/body/eval_jaxpr/all_gather | solution.py:60
  376.6 0.8 compare_select_fusion.3
  378.2 1.2 convolution_bitcast_fusion.4
  379.4 36.6 %all_gather.16 = bf16[64,4096]{1,0:T(8,128)(2,1)S(1)} all-gather(bf16[64,256]{1,0:T(8,128)(2,1)S(1)} %fusion.65), channel_id=1, replica_groups=mesh['chain'=4,'mesh'=16,'probe'=4] {'mesh'}, dimensions={1}, use_global_device_ids=true | all-gather | bytes 557056 | tf_op jit(solution)/shard_map/while/body/eval_jaxpr/all_gather | solution.py:44
  416.0 2.3 fusion.66
  418.3 35.2 %all_gather.17 = bf16[64,4096]{1,0:T(8,128)(2,1)S(1)} all-gather(bf16[64,256]{1,0:T(8,128)(2,1)S(1)} %fusion.66), channel_id=1, replica_groups=mesh['chain'=4,'mesh'=16,'probe'=4] {'mesh'}, dimensions={1}, use_global_device_ids=true | all-gather | bytes 557056 | tf_op jit(solution)/shard_map/while/body/eval_jaxpr/all_gather | solution.py:48
  454.5 36.6 %all_gather.18 = bf16[64,4096]{1,0:T(8,128)(2,1)S(1)} all-gather(bf16[64,256]{1,0:T(8,128)(2,1)S(1)} %fusion.67), channel_id=1, replica_groups=mesh['chain'=4,'mesh'=16,'probe'=4] {'mesh'}, dimensions={1}, use_global_device_ids=true | all-gather | bytes 557056 | tf_op jit(solution)/shard_map/while/body/eval_jaxpr/all_gather | solution.py:44
  491.1 2.3 fusion.68
  493.4 29.6 %collective-permute-start = (bf16[64,256]{1,0:T(8,128)(2,1)S(1)}, bf16[64,256]{1,0:T(8,128)(2,1)S(1)}, u32[]{:S(2)}, u32[]{:S(2)}) collective-permute-start(bf16[64,256]{1,0:T(8,128)(2,1)S(1)} %fusion.68), channel_id=1, source_target_pairs={{0,64},{64,128},{128,192},{1,65},{65,129},{129,193},{2,66},{66,130... | collective-permute-start | bytes 98312 | tf_op jit(solution)/shard_map/while/body/eval_jaxpr/ppermute | solution.py:14
  524.1 35.9 %all_gather.19 = bf16[64,4096]{1,0:T(8,128)(2,1)S(1)} all-gather(bf16[64,256]{1,0:T(8,128)(2,1)S(1)} %collective-permute-done), channel_id=1, replica_groups=mesh['chain'=4,'mesh'=16,'probe'=4] {'mesh'}, dimensions={1}, use_global_device_ids=true | all-gather | bytes 557056 | tf_op jit(solution)/shard_map/while/body/eval_jaxpr/all_gather | solution.py:60
  560.0 0.8 compare_select_fusion.3
  561.7 1.2 convolution_bitcast_fusion.4
  562.8 36.6 %all_gather.16 = bf16[64,4096]{1,0:T(8,128)(2,1)S(1)} all-gather(bf16[64,256]{1,0:T(8,128)(2,1)S(1)} %fusion.65), channel_id=1, replica_groups=mesh['chain'=4,'mesh'=16,'probe'=4] {'mesh'}, dimensions={1}, use_global_device_ids=true | all-gather | bytes 557056 | tf_op jit(solution)/shard_map/while/body/eval_jaxpr/all_gather | solution.py:44
  599.4 2.3 fusion.66
  601.8 34.6 %all_gather.17 = bf16[64,4096]{1,0:T(8,128)(2,1)S(1)} all-gather(bf16[64,256]{1,0:T(8,128)(2,1)S(1)} %fusion.66), channel_id=1, replica_groups=mesh['chain'=4,'mesh'=16,'probe'=4] {'mesh'}, dimensions={1}, use_global_device_ids=true | all-gather | bytes 557056 | tf_op jit(solution)/shard_map/while/body/eval_jaxpr/all_gather | solution.py:48
  637.4 37.1 %all_gather.18 = bf16[64,4096]{1,0:T(8,128)(2,1)S(1)} all-gather(bf16[64,256]{1,0:T(8,128)(2,1)S(1)} %fusion.67), channel_id=1, replica_groups=mesh['chain'=4,'mesh'=16,'probe'=4] {'mesh'}, dimensions={1}, use_global_device_ids=true | all-gather | bytes 557056 | tf_op jit(solution)/shard_map/while/body/eval_jaxpr/all_gather | solution.py:44
  674.4 2.3 fusion.68
  676.8 28.6 %collective-permute-start = (bf16[64,256]{1,0:T(8,128)(2,1)S(1)}, bf16[64,256]{1,0:T(8,128)(2,1)S(1)}, u32[]{:S(2)}, u32[]{:S(2)}) collective-permute-start(bf16[64,256]{1,0:T(8,128)(2,1)S(1)} %fusion.68), channel_id=1, source_target_pairs={{0,64},{64,128},{128,192},{1,65},{65,129},{129,193},{2,66},{66,130... | collective-permute-start | bytes 98312 | tf_op jit(solution)/shard_map/while/body/eval_jaxpr/ppermute | solution.py:14
  706.4 37.4 %all_gather.19 = bf16[64,4096]{1,0:T(8,128)(2,1)S(1)} all-gather(bf16[64,256]{1,0:T(8,128)(2,1)S(1)} %collective-permute-done), channel_id=1, replica_groups=mesh['chain'=4,'mesh'=16,'probe'=4] {'mesh'}, dimensions={1}, use_global_device_ids=true | all-gather | bytes 557056 | tf_op jit(solution)/shard_map/while/body/eval_jaxpr/all_gather | solution.py:60
  743.8 0.9 fusion.19
  744.8 1.6 convolution_add_fusion
  746.5 155.3 %all-reduce.4.cloned.1.call-done = f32[64,512]{1,0:T(8,128)} async-done(((f32[64,512]{1,0:T(8,128)}), f32[64,512]{1,0:T(8,128)}) %all-reduce.4.cloned.1.call-update) | async-done | bytes 131088 | tf_op jit(solution)/shard_map/psum | solution.py:76
  901.8 1.5 copy.24
  903.3 0.9 multiply_reduce_fusion.1
  904.2 50.0 %all-reduce.6.cloned.1.call-done = f32[64,512]{1,0:T(8,128)} async-done(((f32[64,512]{1,0:T(8,128)}), f32[64,512]{1,0:T(8,128)}) %all-reduce.6.cloned.1.call-update) | async-done | bytes 131088 | tf_op jit(solution)/shard_map/psum | solution.py:76
  954.2 1.8 multiply_reduce_fusion
  956.0 8.4 all-reduce
  (72 shorter events, 11.4 us)
Async XLA Ops:
  7.2 947.0 %copy-start = (bf16[512,512]{1,0:T(8,128)(2,1)S(1)}, bf16[512,512]{1,0:T(8,128)(2,1)}, u32[]{:S(2)}) copy-start(bf16[512,512]{1,0:T(8,128)(2,1)} %param.15) | copy-start | bytes 1572868
  7.2 894.6 %all-reduce.4.cloned.1.call-start = ((), (), s32[]{:S(2)}) async-start(), calls=%async_computation | async-start | bytes 262144 | tf_op jit(solution)/shard_map/psum | solution.py:76
  8.3 735.6 %copy-start.2 = (bf16[2,512,256]{2,1,0:T(8,128)(2,1)S(1)}, bf16[2,512,256]{2,1,0:T(8,128)(2,1)}, u32[]{:S(2)}) copy-start(bf16[2,512,256]{2,1,0:T(8,128)(2,1)} %param.14) | copy-start | bytes 1572868
  8.3 945.9 %copy-start.3 = (s32[64,512]{1,0:T(8,128)S(1)}, s32[64,512]{1,0:T(8,128)}, u32[]{:S(2)}) copy-start(s32[64,512]{1,0:T(8,128)} %param.10) | copy-start | bytes 393220
  8.3 85.5 %copy-start.1 = (bf16[2,2,4,128,128]{4,3,2,1,0:T(8,128)(2,1)S(1)}, bf16[2,2,4,128,128]{4,3,2,1,0:T(8,128)(2,1)}, u32[]{:S(2)}) copy-start(bf16[2,2,4,128,128]{4,3,2,1,0:T(8,128)(2,1)} %get-tuple-element.139) | copy-start | bytes 1572868 | tf_op jit(solution)/shard_map/while
  132.4 25.8 %collective-permute-start = (bf16[64,256]{1,0:T(8,128)(2,1)S(1)}, bf16[64,256]{1,0:T(8,128)(2,1)S(1)}, u32[]{:S(2)}, u32[]{:S(2)}) collective-permute-start(bf16[64,256]{1,0:T(8,128)(2,1)S(1)} %fusion.68), channel_id=1, source_target_pairs={{0,64},{64,128},{128,192},{1,65},{65,129},{129,193},{2,66},{66,130... | collective-permute-start | bytes 98312 | tf_op jit(solution)/shard_map/while/body/eval_jaxpr/ppermute | solution.py:14
  194.9 76.9 %copy-start.1 = (bf16[2,2,4,128,128]{4,3,2,1,0:T(8,128)(2,1)S(1)}, bf16[2,2,4,128,128]{4,3,2,1,0:T(8,128)(2,1)}, u32[]{:S(2)}) copy-start(bf16[2,2,4,128,128]{4,3,2,1,0:T(8,128)(2,1)} %get-tuple-element.139) | copy-start | bytes 1572868 | tf_op jit(solution)/shard_map/while
  310.4 31.1 %collective-permute-start = (bf16[64,256]{1,0:T(8,128)(2,1)S(1)}, bf16[64,256]{1,0:T(8,128)(2,1)S(1)}, u32[]{:S(2)}, u32[]{:S(2)}) collective-permute-start(bf16[64,256]{1,0:T(8,128)(2,1)S(1)} %fusion.68), channel_id=1, source_target_pairs={{0,64},{64,128},{128,192},{1,65},{65,129},{129,193},{2,66},{66,130... | collective-permute-start | bytes 98312 | tf_op jit(solution)/shard_map/while/body/eval_jaxpr/ppermute | solution.py:14
  376.6 77.7 %copy-start.1 = (bf16[2,2,4,128,128]{4,3,2,1,0:T(8,128)(2,1)S(1)}, bf16[2,2,4,128,128]{4,3,2,1,0:T(8,128)(2,1)}, u32[]{:S(2)}) copy-start(bf16[2,2,4,128,128]{4,3,2,1,0:T(8,128)(2,1)} %get-tuple-element.139) | copy-start | bytes 1572868 | tf_op jit(solution)/shard_map/while
  493.4 30.6 %collective-permute-start = (bf16[64,256]{1,0:T(8,128)(2,1)S(1)}, bf16[64,256]{1,0:T(8,128)(2,1)S(1)}, u32[]{:S(2)}, u32[]{:S(2)}) collective-permute-start(bf16[64,256]{1,0:T(8,128)(2,1)S(1)} %fusion.68), channel_id=1, source_target_pairs={{0,64},{64,128},{128,192},{1,65},{65,129},{129,193},{2,66},{66,130... | collective-permute-start | bytes 98312 | tf_op jit(solution)/shard_map/while/body/eval_jaxpr/ppermute | solution.py:14
  560.0 77.1 %copy-start.1 = (bf16[2,2,4,128,128]{4,3,2,1,0:T(8,128)(2,1)S(1)}, bf16[2,2,4,128,128]{4,3,2,1,0:T(8,128)(2,1)}, u32[]{:S(2)}) copy-start(bf16[2,2,4,128,128]{4,3,2,1,0:T(8,128)(2,1)} %get-tuple-element.139) | copy-start | bytes 1572868 | tf_op jit(solution)/shard_map/while
  676.8 29.6 %collective-permute-start = (bf16[64,256]{1,0:T(8,128)(2,1)S(1)}, bf16[64,256]{1,0:T(8,128)(2,1)S(1)}, u32[]{:S(2)}, u32[]{:S(2)}) collective-permute-start(bf16[64,256]{1,0:T(8,128)(2,1)S(1)} %fusion.68), channel_id=1, source_target_pairs={{0,64},{64,128},{128,192},{1,65},{65,129},{129,193},{2,66},{66,130... | collective-permute-start | bytes 98312 | tf_op jit(solution)/shard_map/while/body/eval_jaxpr/ppermute | solution.py:14
  746.4 207.7 %all-reduce.6.cloned.1.call-start = ((), (), s32[]{:S(2)}) async-start(), calls=%async_computation.1 | async-start | bytes 262144 | tf_op jit(solution)/shard_map/psum | solution.py:76
Sparse Core Ops, SparseCore 0:
  746.6 155.1 all-reduce.3
  904.5 49.5 all-reduce.5
where the time goes:
time: 974 us; the launch traced here: 972 us
  blocking collectives  593 us (61%)
  waiting for transfers between devices  207 us (21%)
  starting transfers between devices  113 us (12%)
  matrix products  28.6 us (3%)
  between operations  14.1 us (1%)
    all_gather x8, blocking collectives, sweep(): lax.all_gather(resid_b, 'mesh', axis=1, tiled=True)  299 us
    psum x2, waiting for transfers between devices, shards(): coupled_border = lax.psum(lax.psum(partial_border, 'mesh'), 'chain')  205 us
    all_gather x4, blocking collectives, turn(): lax.all_gather(as_sent(moved), 'mesh', axis=1, tiled=True)  145 us
    all_gather x4, blocking collectives, sweep(): prev = lax.all_gather(solved_now, 'mesh', axis=1, tiled=True)  140 us
    ppermute x4, starting transfers between devices, shifted(): lax.ppermute(value, axis, [(source, source + steps) for source in range(f...  113 us
  transfers between devices with their start and end apart: 6, of which 6 were waited for; matrix products, arithmetic and copies ran while one was open for 1% of the time, Pallas kernels for 0%

commit v1 on v0

v1 whole, which is shorter than its diff:
```python
import functools

import jax
import jax.numpy as jnp
from jax import lax
from jax.experimental import pallas as pl
from jax.experimental.pallas import tpu as pltpu
from jax.sharding import Mesh, PartitionSpec as P

AXES = ("zl", "core", "zh", "y", "x")
CHAIN, NODES = ("zl", "core"), ("zh", "y")
NT = (((1,), (1,)), ((), ()))
CHUNKS = 4


def couple_kernel(cols, who, x_ref, own_c, other_c, s_ref, out_ref, c_buf, sem, *, step):
    rows, slots, block = c_buf.shape[0], c_buf.shape[1], c_buf.shape[2]
    mine = pltpu.make_async_copy(own_c.at[step % 2], c_buf, sem)
    theirs = pltpu.make_async_copy(other_c.at[step % 2], c_buf, sem)

    @pl.when(who[0] == step // 2)
    def _():
        mine.start()

    @pl.when(who[0] != step // 2)
    def _():
        theirs.start()

    mine.wait()
    per = x_ref.shape[2] // block
    for row in range(rows):
        total = None
        for slot in range(slots):
            col = cols[(step * rows + row) * slots + slot]
            lanes = pl.ds(pl.multiple_of((col % per) * block, block), block)
            term = lax.dot_general(
                x_ref[col // per, :, lanes], c_buf[row, slot], NT, preferred_element_type=jnp.float32
            )
            total = term if total is None else total + term
        span = slice(row * block, (row + 1) * block)
        resid = (s_ref[:, span] - total).astype(jnp.bfloat16)
        for peer in range(out_ref.shape[0]):
            out_ref[peer, :, span] = resid


def apply_kernel(who, r_ref, own_l, other_l, out_ref, spread_ref, l_buf, sems, *, step):
    width = l_buf.shape[2]

    def copies(source):
        return [
            pltpu.make_async_copy(
                source.at[step % 2, :, pl.ds(i * width, width)], l_buf.at[i], sems.at[i]
            )
            for i in range(CHUNKS)
        ]

    mine, theirs = copies(own_l), copies(other_l)

    @pl.when(who[0] == step // 2)
    def _():
        for copy in mine:
            copy.start()

    @pl.when(who[0] != step // 2)
    def _():
        for copy in theirs:
            copy.start()

    peers, _, piece = r_ref.shape
    total = None
    for i in range(CHUNKS):
        mine[i].wait()
        per = peers // CHUNKS
        left = jnp.concatenate([r_ref[i * per + p] for p in range(per)], axis=1)
        term = lax.dot_general(left, l_buf[i], NT, preferred_element_type=jnp.float32)
        total = term if total is None else total + term
    result = total.astype(jnp.bfloat16)
    out_ref[...] = result
    if spread_ref is not None:
        for peer in range(peers):
            spread_ref[peer] = result


def vmem():
    return pl.BlockSpec(memory_space=pltpu.VMEM)


def smem():
    return pl.BlockSpec(memory_space=pltpu.SMEM)


def hbm():
    return pl.BlockSpec(memory_space=pl.ANY)


def couple(cols, who, pieces, own_c, other_c, source, step):
    peers, probes, piece = pieces.shape
    return pl.pallas_call(
        functools.partial(couple_kernel, step=step),
        out_shape=jax.ShapeDtypeStruct((peers, probes, piece), jnp.bfloat16),
        in_specs=[smem(), smem(), vmem(), hbm(), hbm(), vmem()],
        out_specs=vmem(),
        scratch_shapes=[pltpu.VMEM(own_c.shape[1:], own_c.dtype), pltpu.SemaphoreType.DMA],
        name=f"couple{step}",
    )(cols, who, pieces, own_c, other_c, source)


def apply_factor(who, pieces, own_l, other_l, step):
    peers, probes, piece = pieces.shape
    rows, width = own_l.shape[1:]
    return pl.pallas_call(
        functools.partial(apply_kernel, step=step),
        out_shape=(
            jax.ShapeDtypeStruct((probes, rows), jnp.bfloat16),
            jax.ShapeDtypeStruct((peers, probes, rows), jnp.bfloat16),
        ),
        in_specs=[smem(), vmem(), hbm(), hbm()],
        out_specs=(vmem(), vmem()),
        scratch_shapes=[
            pltpu.VMEM((CHUNKS, rows, width // CHUNKS), own_l.dtype),
            pltpu.SemaphoreType.DMA((CHUNKS,)),
        ],
        compiler_params=pltpu.CompilerParams(vmem_limit_bytes=24 << 20),
        name=f"apply{step}",
    )(who, pieces, own_l, other_l)


def exchange(spread):
    return lax.all_to_all(spread, NODES, 0, 0)


def shards(
    signs, border_signs, inverse_factors, couplings, coupling_cols, border_rows, border_inverse
):
    local_probes, own_steps, local = signs.shape
    cores = lax.axis_size("core")
    peers = lax.axis_size("zh") * lax.axis_size("y")
    probes = local_probes // cores
    steps = own_steps * cores
    core = lax.axis_index("core")
    first = core == 0
    who = jnp.reshape(core, (1,)).astype(jnp.int32)

    def swap(value):
        return lax.ppermute(value, "core", [(0, 1), (1, 0)])

    def in_order(own, other):
        return jnp.concatenate([jnp.where(first, own, other), jnp.where(first, other, own)], axis=0)

    source = (2 * signs - 1).astype(jnp.bfloat16).reshape(cores, probes, own_steps, local)
    source = source.transpose(0, 2, 1, 3)
    own_source = jnp.where(first, source[0], source[1])
    other_source = swap(jnp.where(first, source[1], source[0]))
    source4 = in_order(own_source, other_source)
    other_l = swap(inverse_factors)
    other_c = swap(couplings)
    cols = in_order(coupling_cols, swap(coupling_cols)).reshape(-1)
    source_f32 = source4.astype(jnp.float32)

    pieces = None
    for turn in range(lax.axis_size("zl")):
        results = []
        for step in range(steps):
            if pieces is None:
                spread = jnp.broadcast_to(source4[step][None], (peers, probes, local))
            else:
                spread = couple(cols, who, pieces, couplings, other_c, source_f32[step], step)
            now, spread_now = apply_factor(who, exchange(spread), inverse_factors, other_l, step)
            results.append(now)
            if step + 1 < steps:
                pieces = exchange(spread_now)
        if turn + 1 < lax.axis_size("zl"):
            moved = lax.ppermute(now, "zl", [(turn, turn + 1)])
            pieces = exchange(jnp.broadcast_to(moved[None], (peers, probes, local)))

    solved4 = jnp.stack(results)
    mine = jnp.where(first, solved4[:own_steps], solved4[own_steps:])
    theirs = swap(jnp.where(first, solved4[own_steps:], solved4[:own_steps]))
    solved = jnp.concatenate([jnp.where(first, mine, theirs), jnp.where(first, theirs, mine)], axis=1)
    solved = solved.transpose(1, 0, 2)

    rows4 = in_order(border_rows, swap(border_rows))
    partial = jnp.zeros((probes, border_rows.shape[1]), jnp.float32)
    for step in range(steps):
        partial = partial + lax.dot_general(results[step], rows4[step], NT, preferred_element_type=jnp.float32)
    group = ("zl",) + NODES
    members = lax.axis_size("zl") * peers
    share = probes // members
    parts = lax.all_to_all(partial.reshape(members, share, -1), group, 0, 0)
    coupled_border = jnp.sum(parts, axis=0)
    at = core * probes + lax.axis_index(group) * share
    border_source = (2 * lax.dynamic_slice_in_dim(border_signs, at, share, 0) - 1).astype(jnp.float32)
    border_resid = (border_source - coupled_border).astype(jnp.bfloat16)
    border_part = lax.dot_general(border_resid, border_inverse, NT, preferred_element_type=jnp.float32)
    whole = CHAIN + NODES
    spread = jnp.broadcast_to(border_part[None], (members * cores,) + border_part.shape)
    gathered = lax.all_to_all(spread, whole, 0, 0)
    gathered = gathered.reshape(lax.axis_size("zl"), cores, peers * share, -1).transpose(1, 0, 2, 3)
    border_solved = gathered.reshape(local_probes, -1)

    total_probes = local_probes * lax.axis_size("x")
    node_sums = jnp.sum(jnp.square(solved.astype(jnp.float32)), axis=0)
    border_sums = jnp.sum(jnp.square(border_solved), axis=0)
    node_sums, border_sums = lax.psum((node_sums, border_sums), "x")
    return solved, border_solved, node_sums / total_probes, border_sums / total_probes


def solution(mesh):
    sizes = mesh.shape
    devices = mesh.devices.reshape(2, sizes["chain"] // 2, 4, sizes["mesh"] // 4, sizes["probe"])
    return jax.shard_map(
        shards,
        mesh=Mesh(devices, AXES),
        in_specs=(
            P("x", CHAIN, NODES),
            P("x", None),
            P(CHAIN, NODES, None),
            P(CHAIN, NODES, None, None, None),
            P(CHAIN, NODES, None),
            P(CHAIN, None, NODES),
            P(),
        ),
        out_specs=(P("x", CHAIN, NODES), P("x", None), P(CHAIN, NODES), P()),
        check_vma=False,
    )
```

time: 974 us -> 360 us (0.37)
  blocking collectives: 593 us -> 172 us
  waiting for transfers between devices: 207 us -> 45.2 us
  starting transfers between devices: 113 us -> 70.9 us
  Pallas kernels: 0 us -> 41.1 us
  matrix products: 28.6 us -> 1.69 us
  local copies, waits for them, and re-layouts: 7.94 us -> 23 us
  between operations: 14.1 us -> 1.01 us
    all_gather x16 -> x0, blocking collectives: 584 us -> none  [the longest x8 299 us: sweep(): lax.all_gather(resid_b, 'mesh', axis=1, tiled=True)]
    psum x2 -> x0, waiting for transfers between devices: 205 us -> none  [shards(): coupled_border = lax.psum(lax.psum(partial_border, 'mesh'), 'chain')]
    all_to_all x0 -> x11, blocking collectives: none -> 164 us  [exchange(): return lax.all_to_all(spread, NODES, 0, 0)]
    ppermute x4 -> x7, starting transfers between devices: 113 us -> 30.7 us  [the longest x6 29.4 us: swap(): return lax.ppermute(value, 'core', [(0, 1), (1, 0)])]
    pallas_call x0 -> x15, Pallas kernels: none -> 41.1 us  [the longest x7 20.7 us: couple(): pl.pallas_call(functools.partial(couple_kernel, step=step), out_shape=jax...]
    all_to_all x0 -> x6, starting transfers between devices: none -> 40.2 us  [the longest x4 21.9 us: exchange(): return lax.all_to_all(spread, NODES, 0, 0)]
    all_to_all x0 -> x6, waiting for transfers between devices: none -> 38.6 us  [the longest x4 28.4 us: exchange(): return lax.all_to_all(spread, NODES, 0, 0)]
    dot_general x19 -> x5, matrix products: 28.6 us -> 1.69 us  [the longest x1 0.95 us: shards(): lax.dot_general(border_resid, border_inverse, NT, preferred_element_type=...]
  transfers between devices with their start and end apart: 6 -> 13, of which waited for: 6 -> 6; matrix products, arithmetic and copies ran while one was open for 1% -> 2% of each run, Pallas kernels for 0% -> 2%
where the time goes in v1:
time: 360 us; the launch traced here: 358 us
  blocking collectives  172 us (48%)
  starting transfers between devices  70.9 us (20%)
  waiting for transfers between devices  45.2 us (13%)
  Pallas kernels  41.1 us (11%)
  local copies, waits for them, and re-layouts  23 us (6%)
    all_to_all x11, blocking collectives, exchange(): return lax.all_to_all(spread, NODES, 0, 0)  164 us
    ppermute x6, starting transfers between devices, swap(): return lax.ppermute(value, 'core', [(0, 1), (1, 0)])  29.4 us
    all_to_all x4, waiting for transfers between devices, exchange(): return lax.all_to_all(spread, NODES, 0, 0)  28.4 us
    all_to_all x4, starting transfers between devices, exchange(): return lax.all_to_all(spread, NODES, 0, 0)  21.9 us
    pallas_call x7, Pallas kernels, couple(): pl.pallas_call(functools.partial(couple_kernel, step=step), out_shape=jax...  20.7 us
    pallas_call x8, Pallas kernels, apply_factor(): pl.pallas_call(functools.partial(apply_kernel, step=step), out_shape=(jax...  20.4 us
    unnamed x28, local copies, waits for them, and re-layouts  18.9 us
    all_to_all x1, starting transfers between devices, shards(): gathered = lax.all_to_all(spread, whole, 0, 0)  14 us
  transfers between devices with their start and end apart: 13, of which 6 were waited for; matrix products, arithmetic and copies ran while one was open for 2% of the time, Pallas kernels for 2%

profile of v1, /device:TPU:1, one launch (start us, length us, event | category | flops | bytes accessed | tf_op | source)
XLA Modules:
  0.0 357.6 jit_solution(17381654609154132860)
XLA Ops:
  0.6 3.3 collective-permute-start.2
  5.1 5.7 %collective-permute-done.1 = bf16[2,32,256]{2,1,0:T(8,128)(2,1)S(1)} collective-permute-done((bf16[2,32,256]{2,1,0:T(8,128)(2,1)S(1)}, bf16[2,32,256]{2,1,0:T(8,128)(2,1)S(1)}, u32[]{:S(2)}, u32[]{:S(2)}) %collective-permute-start.1) | collective-permute-done | bytes 32800 | tf_op jit(solution)/shard_map/ppermute | solution.py:145
  11.6 9.2 %all-to-all-start = ((bf16[16,32,256]{2,1,0:T(8,128)(2,1)}), bf16[16,32,256]{2,1,0:T(8,128)(2,1)S(1)}, u32[]{:S(2)}, u32[]{:S(2)}) async-start(bf16[16,32,256]{2,1,0:T(8,128)(2,1)} %broadcast_in_dim.9), calls=%async_computation | async-start | bytes 524288 | tf_op jit(solution)/shard_map/all_to_all | solution.py:129
  21.6 9.9 %all-to-all-done.r_ref = bf16[16,32,256]{2,1,0:T(8,128)(2,1)S(1)} async-done(((bf16[16,32,256]{2,1,0:T(8,128)(2,1)}), bf16[16,32,256]{2,1,0:T(8,128)(2,1)S(1)}, u32[]{:S(2)}, u32[]{:S(2)}) %all-to-all-start) | async-done | bytes 262176 | tf_op jit(solution)/shard_map/all_to_all | solution.py:129
  31.5 2.2 copy-done.1
  33.7 3.3 apply0.2
  37.0 5.1 %all-to-all-start.1 = ((bf16[16,32,256]{2,1,0:T(8,128)(2,1)}), bf16[16,32,256]{2,1,0:T(8,128)(2,1)S(1)}, u32[]{:S(2)}, u32[]{:S(2)}) async-start(bf16[16,32,256]{2,1,0:T(8,128)(2,1)} %get-tuple-element.15), calls=%async_computation.1 | async-start | bytes 524288 | tf_op jit(solution)/shard_map/all_to_all | solution.py:129
  43.4 8.9 %all-to-all-done.1.x_ref = bf16[16,32,256]{2,1,0:T(8,128)(2,1)S(1)} async-done(((bf16[16,32,256]{2,1,0:T(8,128)(2,1)}), bf16[16,32,256]{2,1,0:T(8,128)(2,1)S(1)}, u32[]{:S(2)}, u32[]{:S(2)}) %all-to-all-start.1) | async-done | bytes 262176 | tf_op jit(solution)/shard_map/all_to_all | solution.py:129
  53.1 3.0 couple1.2
  56.0 16.3 %all_to_all.85.r_ref = bf16[16,32,256]{2,1,0:T(8,128)(2,1)S(1)} all-to-all(bf16[16,32,256]{2,1,0:T(8,128)(2,1)} %couple1.2), channel_id=1, replica_groups=mesh['zl'=2,'core'=2,'zh'=4,'y'=4,'x'=4] {'zh','y'}, dimensions={0} | all-to-all | bytes 524288 | tf_op jit(solution)/shard_map/all_to_all | solution.py:129
  72.3 2.2 copy-done.2
  74.5 3.2 apply1.2
  77.7 17.1 %all_to_all.86.x_ref = bf16[16,32,256]{2,1,0:T(8,128)(2,1)} all-to-all(bf16[16,32,256]{2,1,0:T(8,128)(2,1)S(1)} %get-tuple-element.16), channel_id=1, replica_groups=mesh['zl'=2,'core'=2,'zh'=4,'y'=4,'x'=4] {'zh','y'}, dimensions={0} | all-to-all | bytes 524288 | tf_op jit(solution)/shard_map/all_to_all | solution.py:129
  94.8 3.0 couple2.2
  97.7 14.8 %all_to_all.87.r_ref = bf16[16,32,256]{2,1,0:T(8,128)(2,1)S(1)} all-to-all(bf16[16,32,256]{2,1,0:T(8,128)(2,1)} %couple2.2), channel_id=1, replica_groups=mesh['zl'=2,'core'=2,'zh'=4,'y'=4,'x'=4] {'zh','y'}, dimensions={0} | all-to-all | bytes 524288 | tf_op jit(solution)/shard_map/all_to_all | solution.py:129
  112.5 2.2 copy-done.3
  114.7 2.2 apply2.2
  116.9 14.4 %all_to_all.88.x_ref = bf16[16,32,256]{2,1,0:T(8,128)(2,1)} all-to-all(bf16[16,32,256]{2,1,0:T(8,128)(2,1)S(1)} %get-tuple-element.17), channel_id=1, replica_groups=mesh['zl'=2,'core'=2,'zh'=4,'y'=4,'x'=4] {'zh','y'}, dimensions={0} | all-to-all | bytes 524288 | tf_op jit(solution)/shard_map/all_to_all | solution.py:129
  131.4 3.0 couple3.2
  134.3 13.4 %all_to_all.89.r_ref = bf16[16,32,256]{2,1,0:T(8,128)(2,1)S(1)} all-to-all(bf16[16,32,256]{2,1,0:T(8,128)(2,1)} %couple3.2), channel_id=1, replica_groups=mesh['zl'=2,'core'=2,'zh'=4,'y'=4,'x'=4] {'zh','y'}, dimensions={0} | all-to-all | bytes 524288 | tf_op jit(solution)/shard_map/all_to_all | solution.py:129
  147.8 2.2 copy-done.4
  149.9 2.3 apply3.2
  154.4 13.9 %all_to_all.90.x_ref = bf16[16,32,256]{2,1,0:T(8,128)(2,1)} all-to-all(bf16[16,32,256]{2,1,0:T(8,128)(2,1)S(1)} %broadcast_in_dim.10), channel_id=1, replica_groups=mesh['zl'=2,'core'=2,'zh'=4,'y'=4,'x'=4] {'zh','y'}, dimensions={0} | all-to-all | bytes 524288 | tf_op jit(solution)/shard_map/all_to_all | solution.py:129
  168.4 3.0 couple0.1
  171.3 14.1 %all_to_all.91.r_ref = bf16[16,32,256]{2,1,0:T(8,128)(2,1)S(1)} all-to-all(bf16[16,32,256]{2,1,0:T(8,128)(2,1)} %couple0.1), channel_id=1, replica_groups=mesh['zl'=2,'core'=2,'zh'=4,'y'=4,'x'=4] {'zh','y'}, dimensions={0} | all-to-all | bytes 524288 | tf_op jit(solution)/shard_map/all_to_all | solution.py:129
  185.4 2.2 copy-done.5
  187.6 2.6 apply0.3
  190.2 13.3 %all_to_all.92.x_ref = bf16[16,32,256]{2,1,0:T(8,128)(2,1)} all-to-all(bf16[16,32,256]{2,1,0:T(8,128)(2,1)S(1)} %get-tuple-element.20), channel_id=1, replica_groups=mesh['zl'=2,'core'=2,'zh'=4,'y'=4,'x'=4] {'zh','y'}, dimensions={0} | all-to-all | bytes 524288 | tf_op jit(solution)/shard_map/all_to_all | solution.py:129
  203.5 3.0 couple1.3
  206.5 13.9 %all_to_all.93.r_ref = bf16[16,32,256]{2,1,0:T(8,128)(2,1)S(1)} all-to-all(bf16[16,32,256]{2,1,0:T(8,128)(2,1)} %couple1.3), channel_id=1, replica_groups=mesh['zl'=2,'core'=2,'zh'=4,'y'=4,'x'=4] {'zh','y'}, dimensions={0} | all-to-all | bytes 524288 | tf_op jit(solution)/shard_map/all_to_all | solution.py:129
  220.4 2.2 copy-done.6
  222.5 2.6 apply1.3
  225.2 13.5 %all_to_all.94.x_ref = bf16[16,32,256]{2,1,0:T(8,128)(2,1)} all-to-all(bf16[16,32,256]{2,1,0:T(8,128)(2,1)S(1)} %get-tuple-element.22), channel_id=1, replica_groups=mesh['zl'=2,'core'=2,'zh'=4,'y'=4,'x'=4] {'zh','y'}, dimensions={0} | all-to-all | bytes 524288 | tf_op jit(solution)/shard_map/all_to_all | solution.py:129
  238.7 3.0 couple2.3
  241.7 3.9 %all-to-all-start.12 = ((bf16[16,32,256]{2,1,0:T(8,128)(2,1)}), bf16[16,32,256]{2,1,0:T(8,128)(2,1)S(1)}, u32[]{:S(2)}, u32[]{:S(2)}) async-start(bf16[16,32,256]{2,1,0:T(8,128)(2,1)} %couple2.3), calls=%async_computation.12 | async-start | bytes 524288 | tf_op jit(solution)/shard_map/all_to_all | solution.py:129
  245.6 14.5 %collective-permute-start.6 = (bf16[2,512,256]{2,1,0:T(8,128)(2,1)S(1)}, bf16[2,512,256]{2,1,0:T(8,128)(2,1)S(1)}, u32[]{:S(2)}, u32[]{:S(2)}) collective-permute-start(bf16[2,512,256]{2,1,0:T(8,128)(2,1)S(1)} %copy-done.11), channel_id=1, source_target_pairs={{0,64},{64,0},{1,65},{65,1},{2,66},{66,2},{3,67},{67,3},{4,68},{68... | collective-permute-start | bytes 1572872 | tf_op jit(solution)/shard_map/ppermute | solution.py:145
  260.1 2.2 copy-done.7
  263.9 19.2 %all_to_all.95.x_ref = bf16[16,32,256]{2,1,0:T(8,128)(2,1)} all-to-all(bf16[16,32,256]{2,1,0:T(8,128)(2,1)S(1)} %get-tuple-element.24), channel_id=1, replica_groups=mesh['zl'=2,'core'=2,'zh'=4,'y'=4,'x'=4] {'zh','y'}, dimensions={0} | all-to-all | bytes 524288 | tf_op jit(solution)/shard_map/all_to_all | solution.py:129
  283.1 3.0 couple3.3
  286.0 3.7 %all-to-all-start.14 = ((bf16[16,32,256]{2,1,0:T(8,128)(2,1)}), bf16[16,32,256]{2,1,0:T(8,128)(2,1)S(1)}, u32[]{:S(2)}, u32[]{:S(2)}) async-start(bf16[16,32,256]{2,1,0:T(8,128)(2,1)} %couple3.3), calls=%async_computation.14 | async-start | bytes 524288 | tf_op jit(solution)/shard_map/all_to_all | solution.py:129
  290.2 9.5 %all-to-all-done.14.r_ref = bf16[16,32,256]{2,1,0:T(8,128)(2,1)S(1)} async-done(((bf16[16,32,256]{2,1,0:T(8,128)(2,1)}), bf16[16,32,256]{2,1,0:T(8,128)(2,1)S(1)}, u32[]{:S(2)}, u32[]{:S(2)}) %all-to-all-start.14) | async-done | bytes 262176 | tf_op jit(solution)/shard_map/all_to_all | solution.py:129
  299.8 2.2 copy-done.8
  302.0 2.5 apply3.3
  305.5 4.2 %all-to-all-start.15 = ((f32[32,1,512]{2,1,0:T(1,128)}), f32[32,1,512]{2,1,0:T(1,128)S(1)}, u32[]{:S(2)}, u32[]{:S(2)}) async-start(f32[32,1,512]{2,1,0:T(1,128)} %copy.21), calls=%async_computation.15 | async-start | bytes 131072 | tf_op jit(solution)/shard_map/all_to_all | solution.py:189
  309.8 10.6 %collective-permute-start.5 = (bf16[2,32,256]{2,1,0:T(8,128)(2,1)S(1)}, bf16[2,32,256]{2,1,0:T(8,128)(2,1)S(1)}, u32[]{:S(2)}, u32[]{:S(2)}) collective-permute-start(bf16[2,32,256]{2,1,0:T(8,128)(2,1)S(1)} %broadcast_select_fusion.5), channel_id=1, source_target_pairs={{0,64},{64,0},{1,65},{65,1},{2,66},{66,2},{3,67},{67,3},{4,68},{68... | collective-permute-start | bytes 98312 | tf_op jit(solution)/shard_map/ppermute | solution.py:145
  322.2 14.0 %all-to-all-start.16 = ((f32[64,1,512]{2,1,0:T(1,128)}), f32[64,1,512]{2,1,0:T(1,128)S(1)}, u32[]{:S(2)}, u32[]{:S(2)}) async-start(f32[64,1,512]{2,1,0:T(1,128)} %broadcast_in_dim.22), calls=%async_computation.16 | async-start | bytes 262144 | tf_op jit(solution)/shard_map/all_to_all | solution.py:197
  337.0 10.3 %all-to-all-done.16 = f32[64,1,512]{2,1,0:T(1,128)S(1)} async-done(((f32[64,1,512]{2,1,0:T(1,128)}), f32[64,1,512]{2,1,0:T(1,128)S(1)}, u32[]{:S(2)}, u32[]{:S(2)}) %all-to-all-start.16) | async-done | bytes 131104 | tf_op jit(solution)/shard_map/all_to_all | solution.py:197
  348.0 8.4 %all-reduce = (f32[2,256]{1,0:T(2,128)S(1)}, f32[512]{0:T(512)S(1)}) all-reduce(f32[2,256]{1,0:T(2,128)S(1)} %multiply_reduce_fusion.1, f32[512]{0:T(512)S(1)} %multiply_reduce_fusion), channel_id=1, replica_groups=mesh['zl'=2,'core'=2,'zh'=4,'y'=4,'x'=4] {'x'}, use_global_device_ids=true, to_apply=%region_2.3 | all-reduce | flops 1024 | bytes 8192 | tf_op jit(solution)/shard_map/psum | solution.py:204
  (62 shorter events, 14.4 us)
Async XLA Ops:
  0.6 319.8 %copy-start = (bf16[512,512]{1,0:T(8,128)(2,1)S(1)}, bf16[512,512]{1,0:T(8,128)(2,1)}, u32[]{:S(2)}) copy-start(bf16[512,512]{1,0:T(8,128)(2,1)} %param.13) | copy-start | bytes 1572868
  0.6 30.8 %collective-permute-start.2 = (bf16[2,256,4096]{2,1,0:T(8,128)(2,1)}, bf16[2,256,4096]{2,1,0:T(8,128)(2,1)}, u32[]{:S(2)}, u32[]{:S(2)}) collective-permute-start(bf16[2,256,4096]{2,1,0:T(8,128)(2,1)} %own_l.15), channel_id=1, source_target_pairs={{0,64},{64,0},{1,65},{65,1},{2,66},{66,2},{3,67},{67,3},{4,68},{68... | collective-permute-start | bytes 12582920 | tf_op jit(solution)/shard_map/ppermute | solution.py:145
  4.9 5.9 %collective-permute-start.1 = (bf16[2,32,256]{2,1,0:T(8,128)(2,1)S(1)}, bf16[2,32,256]{2,1,0:T(8,128)(2,1)S(1)}, u32[]{:S(2)}, u32[]{:S(2)}) collective-permute-start(bf16[2,32,256]{2,1,0:T(8,128)(2,1)S(1)} %select_bitcast_fusion), channel_id=1, source_target_pairs={{0,64},{64,0},{1,65},{65,1},{2,66},{66,2},{3,67},{67,3},{4,68},{68... | collective-permute-start | bytes 98312 | tf_op jit(solution)/shard_map/ppermute | solution.py:145
  11.6 19.9 %all-to-all-start = ((bf16[16,32,256]{2,1,0:T(8,128)(2,1)}), bf16[16,32,256]{2,1,0:T(8,128)(2,1)S(1)}, u32[]{:S(2)}, u32[]{:S(2)}) async-start(bf16[16,32,256]{2,1,0:T(8,128)(2,1)} %broadcast_in_dim.9), calls=%async_computation | async-start | bytes 524288 | tf_op jit(solution)/shard_map/all_to_all | solution.py:129
  20.7 21.4 %collective-permute-start = (s32[2,2,4]{2,1,0:T(2,128)}, s32[2,2,4]{2,1,0:T(2,128)S(1)}, u32[]{:S(2)}, u32[]{:S(2)}) collective-permute-start(s32[2,2,4]{2,1,0:T(2,128)} %param.11), channel_id=1, source_target_pairs={{0,64},{64,0},{1,65},{65,1},{2,66},{66,2},{3,67},{67,3},{4,68},{68... | collective-permute-start | bytes 200 | tf_op jit(solution)/shard_map/ppermute | solution.py:145
  21.5 21.9 %collective-permute-start.3 = (bf16[2,2,4,128,128]{4,3,2,1,0:T(8,128)(2,1)}, bf16[2,2,4,128,128]{4,3,2,1,0:T(8,128)(2,1)S(1)}, u32[]{:S(2)}, u32[]{:S(2)}) collective-permute-start(bf16[2,2,4,128,128]{4,3,2,1,0:T(8,128)(2,1)} %own_c.13), channel_id=1, source_target_pairs={{0,64},{64,0},{1,65},{65,1},{2,66},{66,2},{3,67},{67,3},{4,68},{68... | collective-permute-start | bytes 1572872 | tf_op jit(solution)/shard_map/ppermute | solution.py:145
  31.5 2.2 copy-start.1
  33.7 8.5 %copy-start.12 = (s32[2,2,4]{2,1,0:T(2,128)S(1)}, s32[2,2,4]{2,1,0:T(2,128)}, u32[]{:S(2)}) copy-start(s32[2,2,4]{2,1,0:T(2,128)} %param.11) | copy-start | bytes 196
  37.0 15.4 %all-to-all-start.1 = ((bf16[16,32,256]{2,1,0:T(8,128)(2,1)}), bf16[16,32,256]{2,1,0:T(8,128)(2,1)S(1)}, u32[]{:S(2)}, u32[]{:S(2)}) async-start(bf16[16,32,256]{2,1,0:T(8,128)(2,1)} %get-tuple-element.15), calls=%async_computation.1 | async-start | bytes 524288 | tf_op jit(solution)/shard_map/all_to_all | solution.py:129
  43.4 8.9 %copy-start.9 = (bf16[2,2,4,128,128]{4,3,2,1,0:T(8,128)(2,1)}, bf16[2,2,4,128,128]{4,3,2,1,0:T(8,128)(2,1)S(1)}, u32[]{:S(2)}) copy-start(bf16[2,2,4,128,128]{4,3,2,1,0:T(8,128)(2,1)S(1)} %collective-permute-done.3.other_c) | copy-start | bytes 1572868
  52.4 0.7 copy-start.10
  72.3 2.2 copy-start.2
  112.5 2.2 copy-start.3
  147.8 2.2 copy-start.4
  152.3 2.1 collective-permute-start.4
  185.4 2.2 copy-start.5
  220.4 2.2 copy-start.6
  222.5 23.0 %copy-start.11 = (bf16[2,512,256]{2,1,0:T(8,128)(2,1)S(1)}, bf16[2,512,256]{2,1,0:T(8,128)(2,1)}, u32[]{:S(2)}) copy-start(bf16[2,512,256]{2,1,0:T(8,128)(2,1)} %param.12) | copy-start | bytes 1572868
  241.7 18.4 %all-to-all-start.12 = ((bf16[16,32,256]{2,1,0:T(8,128)(2,1)}), bf16[16,32,256]{2,1,0:T(8,128)(2,1)S(1)}, u32[]{:S(2)}, u32[]{:S(2)}) async-start(bf16[16,32,256]{2,1,0:T(8,128)(2,1)} %couple2.3), calls=%async_computation.12 | async-start | bytes 524288 | tf_op jit(solution)/shard_map/all_to_all | solution.py:129
  245.6 44.2 %collective-permute-start.6 = (bf16[2,512,256]{2,1,0:T(8,128)(2,1)S(1)}, bf16[2,512,256]{2,1,0:T(8,128)(2,1)S(1)}, u32[]{:S(2)}, u32[]{:S(2)}) collective-permute-start(bf16[2,512,256]{2,1,0:T(8,128)(2,1)S(1)} %copy-done.11), channel_id=1, source_target_pairs={{0,64},{64,0},{1,65},{65,1},{2,66},{66,2},{3,67},{67,3},{4,68},{68... | collective-permute-start | bytes 1572872 | tf_op jit(solution)/shard_map/ppermute | solution.py:145
  260.1 2.2 copy-start.7
  286.0 13.7 %all-to-all-start.14 = ((bf16[16,32,256]{2,1,0:T(8,128)(2,1)}), bf16[16,32,256]{2,1,0:T(8,128)(2,1)S(1)}, u32[]{:S(2)}, u32[]{:S(2)}) async-start(bf16[16,32,256]{2,1,0:T(8,128)(2,1)} %couple3.3), calls=%async_computation.14 | async-start | bytes 524288 | tf_op jit(solution)/shard_map/all_to_all | solution.py:129
  299.8 2.2 copy-start.8
  305.5 14.9 %all-to-all-start.15 = ((f32[32,1,512]{2,1,0:T(1,128)}), f32[32,1,512]{2,1,0:T(1,128)S(1)}, u32[]{:S(2)}, u32[]{:S(2)}) async-start(f32[32,1,512]{2,1,0:T(1,128)} %copy.21), calls=%async_computation.15 | async-start | bytes 131072 | tf_op jit(solution)/shard_map/all_to_all | solution.py:189
  309.8 26.4 %collective-permute-start.5 = (bf16[2,32,256]{2,1,0:T(8,128)(2,1)S(1)}, bf16[2,32,256]{2,1,0:T(8,128)(2,1)S(1)}, u32[]{:S(2)}, u32[]{:S(2)}) collective-permute-start(bf16[2,32,256]{2,1,0:T(8,128)(2,1)S(1)} %broadcast_select_fusion.5), channel_id=1, source_target_pairs={{0,64},{64,0},{1,65},{65,1},{2,66},{66,2},{3,67},{67,3},{4,68},{68... | collective-permute-start | bytes 98312 | tf_op jit(solution)/shard_map/ppermute | solution.py:145
  322.2 25.1 %all-to-all-start.16 = ((f32[64,1,512]{2,1,0:T(1,128)}), f32[64,1,512]{2,1,0:T(1,128)S(1)}, u32[]{:S(2)}, u32[]{:S(2)}) async-start(f32[64,1,512]{2,1,0:T(1,128)} %broadcast_in_dim.22), calls=%async_computation.16 | async-start | bytes 262144 | tf_op jit(solution)/shard_map/all_to_all | solution.py:197
